TPU v7x, 32 devices: a whole 2x2x4 slice. The times are simulated.
32 devices in a mesh: group: 8 (over z, x), inner: 4 (over y, core).
Axes of the slice: x: 2, y: 2, z: 4, core: 2. Of those that a mesh axis runs over, the one named last changes fastest.
Arguments:
- state: float32 [2, 4194304], P(None, ('group', 'inner')), may hold values from -6 to 6
- gates: float32 [8, 2, 128, 128], replicated, may hold values from -0.375 to 0.375
Outputs:
- evolved: float32 [2, 4194304], P(None, ('group', 'inner'))
All inputs are finite; a program needn't handle non-finite values.
Results may differ from a plain program's by a relative error of at most 0.000073.
Values sent between devices are 32-bit elements; how exact they have to be, the bound alone decides.
A program may use at most 64 MiB of HBM per device.

v0:
```python
import jax
import jax.numpy as jnp
from jax import lax
from jax.sharding import PartitionSpec as P


def apply_gate(state, mixer, start):
    size = mixer.shape[-1]
    total = state.shape[1]
    real_part = mixer[0]
    imag_part = mixer[1]
    block = jnp.stack(
        [jnp.stack([real_part, -imag_part], 1), jnp.stack([imag_part, real_part], 1)], 0
    )
    if start == 0:
        view = state.reshape(2, total // size, size)
        result = jnp.einsum("ckdj,daj->cak", block, view, precision=lax.Precision.HIGHEST)
    else:
        view = state.reshape(2, total // (size << start), size, 1 << start)
        result = jnp.einsum("ckdj,dajb->cakb", block, view, precision=lax.Precision.HIGHEST)
    return result.reshape(2, total)


def body(state, gates):
    n_inner = lax.axis_size("inner")
    n_group = lax.axis_size("group")
    total = state.shape[1]
    size = gates.shape[-1]
    local_bits = total.bit_length() - 1
    gate_bits = size.bit_length() - 1
    inner_bits = n_inner.bit_length() - 1
    upper = local_bits - gate_bits
    amps = apply_gate(state, gates[0], 0)
    amps = apply_gate(amps, gates[1], upper)
    low_gate = gates[3]
    shaped = amps.reshape(2, n_inner, total // (n_inner * size), size)
    pieces = lax.all_to_all(shaped, "inner", split_axis=1, concat_axis=1, tiled=True)
    amps = apply_gate(pieces.reshape(2, -1), low_gate, 0).reshape(pieces.shape).reshape(2, total)
    amps = apply_gate(amps, gates[2], upper)
    shaped = amps.reshape(2, n_inner, n_group, total // (n_inner * n_group))
    amps = lax.all_to_all(shaped, "group", split_axis=2, concat_axis=2, tiled=True).reshape(
        2, total
    )
    amps = apply_gate(amps, gates[4], upper - inner_bits)
    amps = apply_gate(amps, gates[5], 0)
    amps = apply_gate(amps, gates[6], upper)
    amps = apply_gate(amps, gates[7], upper // 2)
    shaped = amps.reshape(2, n_inner, n_group, total // (n_inner * n_group))
    shaped = lax.all_to_all(shaped, "group", split_axis=2, concat_axis=2, tiled=True)
    shaped = lax.all_to_all(shaped, "inner", split_axis=1, concat_axis=1, tiled=True)
    return shaped.reshape(2, total)


def solution(mesh):
    in_specs = (P(None, ("group", "inner")), P())
    out_specs = P(None, ("group", "inner"))
    return jax.shard_map(body, mesh=mesh, in_specs=in_specs, out_specs=out_specs, check_vma=False)
```

profile of v0, /device:TPU:0, one launch (start us, length us, event | category | flops | bytes accessed | tf_op | source)
XLA Modules:
  0.0 139.3 jit_solution(9878729280810959320)
XLA Ops:
  0.0 0.0 copy-start
  0.0 1.8 %fusion.48 = (f32[128,1,128]{2,0,1:T(8,128)S(1)}, f32[128,1,128]{2,0,1:T(8,128)S(1)}, f32[128,1,128]{2,0,1:T(8,128)S(1)}, f32[128,1,128]{2,0,1:T(8,128)}, f32[12...) fusion(f32[8,2,128,128]{3,2,1,0:T(8,128)} %param.3), kind=kLoop, calls=%fused_computation.88 | loop fusion | flops 131072 | bytes 1048576 | tf_op jit(solution)/shard_map/neg | solution.py:13
  1.8 2.0 %slice_bitcast_fusion = (f32[128,1,128]{2,0,1:T(8,128)S(1)}, f32[128,1,128]{2,0,1:T(8,128)S(1)}, f32[128,1,128]{2,0,1:T(8,128)S(1)}, f32[128,1,128]{2,0,1:T(8,12...) fusion(f32[8,2,128,128]{3,2,1,0:T(8,128)} %param.3), kind=kLoop, calls=%fused_computation.57 | loop fusion | bytes 2097152 | tf_op jit(solution)/shard_map/squeeze | solution.py:11
  3.9 0.0 copy-done
  3.9 1.1 convolution_bitcast_fusion.6
  5.0 0.3 copy.33
  5.3 0.2 reshape.142
  5.5 1.8 %convolution_bitcast_fusion.5 = f32[2,1,128,1024]{2,3,0,1:T(8,128)S(1)} fusion(f32[2,128,1024]{2,1,0:T(8,128)S(1)} %reshape.142, f32[1,128,2,128]{3,1,2,0:T(8,128)S(1)} %get-tuple-element.45, f32[1,128,2,128]{3,1,2,0:T(8,128)S(1)} %get-tuple-element.46), kind=kOutput, calls=%fused_computation.8 | convolution fusion | flops 805371904 | bytes 2359296 | tf_op jit(solution)/shard_map/ckdj,dajb->cakb/dot_general | solution.py:20
  7.3 0.0 copy-start.7
  7.3 0.0 copy-start.8
  7.3 0.0 copy-start.9
  7.3 0.0 copy-start.2
  7.3 0.0 copy-start.3
  7.4 0.3 copy.35
  7.7 0.2 reshape_reshape.23
  7.9 1.0 copy.36
  8.9 4.3 %all-to-all-start = ((f32[2,4,256,128]{3,2,0,1:T(8,128)}), f32[2,4,256,128]{3,2,0,1:T(8,128)S(1)}, u32[]{:S(2)}, u32[]{:S(2)}) async-start(f32[2,4,256,128]{3,2,0,1:T(8,128)} %copy.36), calls=%async_computation | async-start | bytes 2097152 | tf_op jit(solution)/shard_map/all_to_all | solution.py:37
  13.2 0.0 copy-done.7
  13.2 0.0 copy-done.8
  13.2 0.0 copy-done.9
  13.2 0.0 copy-done.2
  13.2 0.0 copy-done.3
  13.3 14.3 %all-to-all-done = f32[2,4,256,128]{3,2,0,1:T(8,128)S(1)} async-done(((f32[2,4,256,128]{3,2,0,1:T(8,128)}), f32[2,4,256,128]{3,2,0,1:T(8,128)S(1)}, u32[]{:S(2)}, u32[]{:S(2)}) %all-to-all-start) | async-done | bytes 1048608 | tf_op jit(solution)/shard_map/all_to_all | solution.py:37
  27.6 0.1 copy.37
  27.7 1.0 convolution_bitcast_fusion.4
  28.7 0.2 reshape.143
  28.9 1.8 %convolution_bitcast_fusion.3 = f32[2,1,128,1024]{2,3,0,1:T(8,128)S(1)} fusion(f32[2,128,1024]{2,1,0:T(8,128)S(1)} %reshape.143, f32[1,128,2,128]{3,1,2,0:T(8,128)S(1)} %get-tuple-element.38, f32[1,128,2,128]{3,1,2,0:T(8,128)S(1)} %get-tuple-element.37), kind=kOutput, calls=%fused_computation.6 | convolution fusion | flops 805371904 | bytes 2359296 | tf_op jit(solution)/shard_map/ckdj,dajb->cakb/dot_general | solution.py:20
  30.7 0.0 copy-start.4
  30.7 0.0 copy-start.5
  30.7 0.0 copy-start.6
  30.7 0.3 copy.39
  31.1 0.5 reshape_reshape.25
  31.5 1.6 %copy.40 = f32[2,4,8,4096]{3,1,0,2:T(4,128)} copy(f32[2,4,8,4096]{3,2,1,0:T(8,128)S(1)} %reshape_reshape.25) | data formatting | bytes 2097152 | tf_op jit(solution)/shard_map/reshape;reshape | solution.py:40
  33.2 6.5 %all-to-all-start.1 = ((f32[2,4,8,4096]{3,1,0,2:T(4,128)}), f32[2,4,8,4096]{3,1,0,2:T(4,128)S(1)}, u32[]{:S(2)}, u32[]{:S(2)}) async-start(f32[2,4,8,4096]{3,1,0,2:T(4,128)} %copy.40), calls=%async_computation.1 | async-start | bytes 2097152 | tf_op jit(solution)/shard_map/all_to_all | solution.py:41
  39.7 0.0 copy-done.4
  39.7 0.0 copy-done.5
  39.7 0.0 copy-done.6
  39.7 0.8 maximum_bitcast_fusion.16
  40.5 24.8 %all-to-all-done.1 = f32[2,4,8,4096]{3,1,0,2:T(4,128)S(1)} async-done(((f32[2,4,8,4096]{3,1,0,2:T(4,128)}), f32[2,4,8,4096]{3,1,0,2:T(4,128)S(1)}, u32[]{:S(2)}, u32[]{:S(2)}) %all-to-all-start.1) | async-done | bytes 1048608 | tf_op jit(solution)/shard_map/all_to_all | solution.py:41
  65.3 0.6 copy.41
  65.9 0.2 reshape_reshape.26
  66.1 1.8 %convolution_bitcast_fusion.2 = f32[2,4,128,256]{2,3,0,1:T(8,128)S(1)} fusion(f32[1,128,2,128]{3,1,2,0:T(8,128)S(1)} %get-tuple-element.36, f32[1,128,2,128]{3,1,2,0:T(8,128)S(1)} %get-tuple-element.35, f32[2,4,128,256]{3,2,1,0:T(8,128)S(1)} %reshape_reshape.26), kind=kOutput, calls=%fused_computation.5 | convolution fusion | flops 805371904 | bytes 2359296 | tf_op jit(solution)/shard_map/ckdj,dajb->cakb/dot_general | solution.py:20
  67.9 0.3 copy.43
  68.2 0.1 reshape.157
  68.3 1.0 convolution_bitcast_fusion.1
  69.3 0.2 reshape.144
  69.5 2.8 %convolution_bitcast_fusion = f32[2,1,128,1024]{2,3,0,1:T(8,128)S(1)} fusion(f32[2,128,1024]{2,1,0:T(8,128)S(1)} %reshape.144, f32[1,128,2,128]{3,1,2,0:T(8,128)} %get-tuple-element.32, f32[1,128,2,128]{3,1,2,0:T(8,128)} %get-tuple-element.31), kind=kOutput, calls=%fused_computation.3 | convolution fusion | flops 805371904 | bytes 2359296 | tf_op jit(solution)/shard_map/ckdj,dajb->cakb/dot_general | solution.py:20
  72.3 0.0 copy-start.1
  72.3 0.3 copy.45
  72.6 2.7 %reshape_reshape.28 = f32[2,32,128,32]{3,2,1,0:T(8,128)} reshape(f32[2,1,128,1024]{3,2,0,1:T(8,128)S(1)} %copy.45) | data formatting | bytes 2097152 | tf_op jit(solution)/shard_map/reshape;reshape | solution.py:19
  75.3 0.0 copy-done.1
  75.4 8.6 %fusion.2 = f32[2,32,128,32]{2,3,0,1:T(8,128)S(1)} fusion(f32[1,128,2,128]{3,1,2,0:T(8,128)S(1)} %get-tuple-element.49, f32[1,128,2,128]{3,1,2,0:T(8,128)S(1)} %copy-done.1, f32[2,32,128,32]{3,2,1,0:T(8,128)} %reshape_reshape.28), kind=kOutput, calls=%fused_computation.2 | convolution fusion | flops 805371904 | bytes 2359296 | tf_op jit(solution)/shard_map/ckdj,dajb->cakb/dot_general | solution.py:20
  83.9 2.7 %copy.47 = f32[2,32,128,32]{3,2,1,0:T(8,128)} copy(f32[2,32,128,32]{2,3,0,1:T(8,128)S(1)} %fusion.2) | data formatting | bytes 2097152 | tf_op jit(solution)/shard_map/ckdj,dajb->cakb/transpose | solution.py:20
  86.6 3.5 %reshape_reshape.29 = f32[2,4,8,4096]{3,2,1,0:T(8,128)S(1)} reshape(f32[2,32,128,32]{3,2,1,0:T(8,128)} %copy.47) | data formatting | bytes 2097152 | tf_op jit(solution)/shard_map/reshape;reshape | solution.py:48
  90.1 0.7 copy.48
  90.8 29.2 %all_to_all.20 = f32[2,4,8,4096]{3,1,0,2:T(4,128)S(1)} all-to-all(f32[2,4,8,4096]{3,1,0,2:T(4,128)S(1)} %copy.48), channel_id=1, replica_groups=mesh['group'=8,'inner'=4] {'group'}, dimensions={2} | all-to-all | bytes 2097152 | tf_op jit(solution)/shard_map/all_to_all | solution.py:49
  120.0 0.6 copy.49
  120.6 16.9 %all_to_all.21 = f32[2,4,8,4096]{3,2,0,1:T(8,128)S(1)} all-to-all(f32[2,4,8,4096]{3,2,0,1:T(8,128)S(1)} %copy.49), channel_id=1, replica_groups=mesh['group'=8,'inner'=4] {'inner'}, dimensions={1} | all-to-all | bytes 2097152 | tf_op jit(solution)/shard_map/all_to_all | solution.py:50
  137.4 0.1 copy.84
  137.5 1.8 %copy.72 = f32[1,2,32,4096]{3,1,2,0:T(2,128)} copy(f32[1,2,32,4096]{3,2,1,0:T(8,128)S(1)} %bitcast.181) | data formatting | bytes 2097152
  (4 shorter events, 0.1 us)
Async XLA Ops:
  0.0 3.9 %copy-start = (f32[2,131072]{1,0:T(2,128)S(1)}, f32[2,131072]{1,0:T(2,128)}, u32[]{:S(2)}) copy-start(f32[2,131072]{1,0:T(2,128)} %param.2) | copy-start | bytes 3145732
  7.3 5.9 %copy-start.7 = (f32[128,1,128]{2,0,1:T(8,128)S(1)}, f32[128,1,128]{2,0,1:T(8,128)}, u32[]{:S(2)}) copy-start(f32[128,1,128]{2,0,1:T(8,128)} %get-tuple-element.10) | copy-start | bytes 196612
  7.3 5.9 %copy-start.8 = (f32[128,1,128]{2,0,1:T(8,128)S(1)}, f32[128,1,128]{2,0,1:T(8,128)}, u32[]{:S(2)}) copy-start(f32[128,1,128]{2,0,1:T(8,128)} %get-tuple-element.22) | copy-start | bytes 196612
  7.3 5.9 %copy-start.9 = (f32[128,1,128]{2,0,1:T(8,128)S(1)}, f32[128,1,128]{2,0,1:T(8,128)}, u32[]{:S(2)}) copy-start(f32[128,1,128]{2,0,1:T(8,128)} %get-tuple-element.23) | copy-start | bytes 196612
  7.3 5.9 %copy-start.2 = (f32[128,1,128]{2,0,1:T(8,128)S(1)}, f32[128,1,128]{2,0,1:T(8,128)}, u32[]{:S(2)}) copy-start(f32[128,1,128]{2,0,1:T(8,128)} %get-tuple-element.20) | copy-start | bytes 196612
  7.3 5.9 %copy-start.3 = (f32[128,1,128]{2,0,1:T(8,128)S(1)}, f32[128,1,128]{2,0,1:T(8,128)}, u32[]{:S(2)}) copy-start(f32[128,1,128]{2,0,1:T(8,128)} %get-tuple-element.21) | copy-start | bytes 196612
  8.9 18.7 %all-to-all-start = ((f32[2,4,256,128]{3,2,0,1:T(8,128)}), f32[2,4,256,128]{3,2,0,1:T(8,128)S(1)}, u32[]{:S(2)}, u32[]{:S(2)}) async-start(f32[2,4,256,128]{3,2,0,1:T(8,128)} %copy.36), calls=%async_computation | async-start | bytes 2097152 | tf_op jit(solution)/shard_map/all_to_all | solution.py:37
  30.7 9.0 %copy-start.4 = (f32[128,1,128]{2,0,1:T(8,128)S(1)}, f32[128,1,128]{2,0,1:T(8,128)}, u32[]{:S(2)}) copy-start(f32[128,1,128]{2,0,1:T(8,128)} %get-tuple-element.8) | copy-start | bytes 196612
  30.7 9.0 %copy-start.5 = (f32[128,1,128]{2,0,1:T(8,128)S(1)}, f32[128,1,128]{2,0,1:T(8,128)}, u32[]{:S(2)}) copy-start(f32[128,1,128]{2,0,1:T(8,128)} %get-tuple-element.18) | copy-start | bytes 196612
  30.7 9.0 %copy-start.6 = (f32[128,1,128]{2,0,1:T(8,128)S(1)}, f32[128,1,128]{2,0,1:T(8,128)}, u32[]{:S(2)}) copy-start(f32[128,1,128]{2,0,1:T(8,128)} %get-tuple-element.19) | copy-start | bytes 196612
  33.2 32.1 %all-to-all-start.1 = ((f32[2,4,8,4096]{3,1,0,2:T(4,128)}), f32[2,4,8,4096]{3,1,0,2:T(4,128)S(1)}, u32[]{:S(2)}, u32[]{:S(2)}) async-start(f32[2,4,8,4096]{3,1,0,2:T(4,128)} %copy.40), calls=%async_computation.1 | async-start | bytes 2097152 | tf_op jit(solution)/shard_map/all_to_all | solution.py:41
  72.3 3.1 %copy-start.1 = (f32[1,128,2,128]{3,1,2,0:T(8,128)S(1)}, f32[1,128,2,128]{3,1,2,0:T(8,128)}, u32[]{:S(2)}) copy-start(f32[1,128,2,128]{3,1,2,0:T(8,128)} %get-tuple-element.50) | copy-start | bytes 393220
where the time goes:
time: 140 us; the launch traced here: 139 us
  blocking collectives  46 us (33%)
  waiting for transfers between devices  39.1 us (28%)
  local copies, waits for them, and re-layouts  20.4 us (15%)
  matrix products  19.9 us (14%)
  starting transfers between devices  10.8 us (8%)
  other arithmetic  2.71 us (2%)
    all_to_all x1, blocking collectives, body(): lax.all_to_all(shaped, 'group', split_axis=2, concat_axis=2, tiled=True)  29.2 us
    all_to_all x1, waiting for transfers between devices, body(): lax.all_to_all(shaped, 'group', split_axis=2, concat_axis=2, tiled=True)  24.8 us
    all_to_all x1, blocking collectives, body(): lax.all_to_all(shaped, 'inner', split_axis=1, concat_axis=1, tiled=True)  16.9 us
    dot_general x5, matrix products, apply_gate(): jnp.einsum('ckdj,dajb->cakb', block, view, precision=lax.Precision.HIGHEST)  16.8 us
    all_to_all x1, waiting for transfers between devices, body(): lax.all_to_all(shaped, 'inner', split_axis=1, concat_axis=1, tiled=True)  14.3 us
    all_to_all x1, starting transfers between devices, body(): lax.all_to_all(shaped, 'group', split_axis=2, concat_axis=2, tiled=True)  6.51 us
    another operation x4, local copies, waits for them, and re-layouts, body(): shaped = amps.reshape(2, n_inner, n_group, total // (n_inner * n_group))  6.3 us
    all_to_all x1, starting transfers between devices, body(): lax.all_to_all(shaped, 'inner', split_axis=1, concat_axis=1, tiled=True)  4.27 us
  transfers between devices with their start and end apart: 2, of which 2 were waited for; matrix products, arithmetic and copies ran while one was open for 1% of the time, Pallas kernels for 0%

commit v1 on v0

--- a/solution.py
+++ b/solution.py
@@ -1,17 +1,25 @@
+import functools
+
 import jax
 import jax.numpy as jnp
 from jax import lax
+from jax.experimental import pallas as pl
+from jax.experimental.pallas import tpu as pltpu
 from jax.sharding import PartitionSpec as P
+
+
+def blocked(mixer):
+    real_part = mixer[0]
+    imag_part = mixer[1]
+    return jnp.stack(
+        [jnp.stack([real_part, -imag_part], 1), jnp.stack([imag_part, real_part], 1)], 0
+    )
 
 
 def apply_gate(state, mixer, start):
     size = mixer.shape[-1]
     total = state.shape[1]
-    real_part = mixer[0]
-    imag_part = mixer[1]
-    block = jnp.stack(
-        [jnp.stack([real_part, -imag_part], 1), jnp.stack([imag_part, real_part], 1)], 0
-    )
+    block = blocked(mixer)
     if start == 0:
         view = state.reshape(2, total // size, size)
         result = jnp.einsum("ckdj,daj->cak", block, view, precision=lax.Precision.HIGHEST)
@@ -21,7 +29,7 @@
     return result.reshape(2, total)
 
 
-def body(state, gates):
+def general_body(state, gates):
     n_inner = lax.axis_size("inner")
     n_group = lax.axis_size("group")
     total = state.shape[1]
@@ -51,7 +59,250 @@
     return shaped.reshape(2, total)
 
 
+F32 = jnp.float32
+BF16 = jnp.bfloat16
+
+
+def split(value):
+    high = value.astype(BF16)
+    return high, (value - high.astype(F32)).astype(BF16)
+
+
+def dot3(left, right, transposed=False):
+    dims = (((1,), (1 if transposed else 0,)), ((), ()))
+    mul = functools.partial(lax.dot_general, dimension_numbers=dims, preferred_element_type=F32)
+    (lh, ll), (rh, rl) = left, right
+    return mul(lh, rh) + (mul(lh, rl) + mul(ll, rh))
+
+
+def exchange(x, axis, pairs):
+    lane = lax.broadcasted_iota(jnp.int32, (1, x.shape[-1]), 1)
+    for lane_bit, bit in pairs:
+        shift = 1 << lane_bit
+        upper = ((lane >> lane_bit) & 1) == 1
+        shape = x.shape
+        y = x.reshape(shape[:axis] + (shape[axis] >> (bit + 1), 2, 1 << bit) + shape[axis + 1 :])
+        cut = (slice(None),) * (axis + 1)
+        a, b = y[cut + (0,)], y[cut + (1,)]
+        rows = a.reshape(-1, shape[-1])
+        ra = pltpu.roll(rows, shape[-1] - shift, 1).reshape(a.shape)
+        rb = pltpu.roll(b.reshape(-1, shape[-1]), shift, 1).reshape(a.shape)
+        first = jnp.where(upper, rb, a)
+        second = jnp.where(upper, b, ra)
+        x = jnp.stack([first, second], axis + 1).reshape(shape)
+    return x
+
+
+def kernel(
+    n_group, n_inner, x_ref, w_ref, o_ref, send1, recv1, send2, recv2, tmp, weights, ssem, rsem
+):
+    devices = n_group * n_inner
+    size = x_ref.shape[1]
+    wide = 2 * size
+    mid = x_ref.shape[0] // wide
+    rest = size // devices
+    low = size // devices
+    half = size // n_group // low
+    seven = mid // half
+    chunks = 2
+    sub = 2 * low
+    group, inner = lax.axis_index("group"), lax.axis_index("inner")
+    me = group * n_inner + inner
+
+    def peer(step):
+        other = lax.rem(me + step, devices)
+        return other, (other // n_inner, lax.rem(other, n_inner))
+
+    barrier = pltpu.get_barrier_semaphore()
+
+    @pl.loop(1, devices)
+    def _(step):
+        pl.semaphore_signal(
+            barrier, inc=1, device_id=peer(step)[1], device_id_type=pl.DeviceIdType.MESH
+        )
+
+    for k in range(w_ref.shape[0]):
+        weights[k, 0], weights[k, 1] = split(w_ref[k])
+
+    def weight(k):
+        return weights[k, 0], weights[k, 1]
+
+    def copies(swap, chunk, step, source, landing):
+        other, where = peer(step)
+        return pltpu.make_async_remote_copy(
+            src_ref=source.at[chunk, other],
+            dst_ref=landing.at[chunk, me],
+            send_sem=ssem.at[swap, chunk, step],
+            recv_sem=rsem.at[swap, chunk, step],
+            device_id=where,
+            device_id_type=pl.DeviceIdType.MESH,
+        )
+
+    def start(swap, chunk, source, landing):
+        @pl.loop(1, devices)
+        def _(step):
+            copies(swap, chunk, step, source, landing).start()
+
+        landing[chunk, me] = source[chunk, me]
+
+    def finish(swap, chunk, source, landing):
+        @pl.loop(1, devices)
+        def _(step):
+            copies(swap, chunk, step, source, landing).wait()
+
+    cols = [
+        jnp.concatenate(
+            [x_ref[pl.ds(2 * q + c, size, stride=2 * mid), :] for c in range(2)], axis=0
+        )
+        for q in range(mid)
+    ]
+    y = dot3(weight(0), split(jnp.concatenate(cols, axis=1)))
+    run = size // (chunks * low)
+    tiles = [
+        y[:, q * size : (q + 1) * size].reshape(2, chunks, low, run, size) for q in range(mid)
+    ]
+    y = jnp.stack(tiles, 3)
+    y = y.reshape(2, chunks, low * size, size)
+    pl.semaphore_wait(barrier, devices - 1)
+    for chunk in range(chunks):
+        rows = jnp.concatenate([y[0, chunk], y[1, chunk]], axis=1)
+        z = dot3(weight(1), split(rows), True)
+        for w in range(low):
+            piece = z[:, w * size : (w + 1) * size].reshape(devices, 2 * rest, size)
+            send1[chunk, :, w * 2 * rest : (w + 1) * 2 * rest, :] = piece
+        start(0, chunk, send1, recv1)
+
+    bits_t = range(n_group.bit_length() - 1)
+    lane_bits = size.bit_length() - 1
+    bits_r = range(rest.bit_length() - 1)
+    top = lane_bits - len(bits_r)
+    pair_tu = [(k, k) for k in bits_t]
+    pair_er = [(top + k, k) for k in bits_r]
+    pair_t7 = [(lane_bits - len(bits_t) + k, k) for k in bits_t]
+
+    def apply(k, x, axis):
+        parts = x.shape[axis]
+        picked = [lax.index_in_dim(x, i, axis, keepdims=False) for i in range(parts)]
+        kept = picked[0].shape
+        flat = jnp.concatenate([p.reshape(wide, size) for p in picked], axis=1)
+        out = dot3(weight(k), split(flat))
+        pieces = [out[:, i * size : (i + 1) * size].reshape(kept) for i in range(parts)]
+        return jnp.stack(pieces, axis)
+
+    for chunk in range(chunks):
+        finish(0, chunk, send1, recv1)
+        flat = recv1.at[chunk].reshape(devices * sub * rest, size)
+        x = jnp.stack([flat[pl.ds(r, devices * sub, stride=rest), :] for r in range(rest)], 0)
+        x = x.reshape(rest, n_group, n_inner, sub, size)
+        x = exchange(x, 1, pair_tu)
+        x = apply(2, x, 0)
+        x = exchange(x, 1, pair_tu)
+        x = exchange(x, 0, pair_er)
+        x = apply(3, x, 2)
+        x = apply(4, x, 0)
+        x = exchange(x, 1, pair_t7)
+        x = apply(5, x, 2)
+        x = exchange(x, 1, pair_t7)
+        x = x.reshape(half, devices, sub, size)
+        for e in range(half):
+            send2[chunk, :, e * sub : (e + 1) * sub, :] = x[e]
+        start(1, chunk, send2, recv2)
+
+    span = x_ref.shape[0] // chunks
+    for chunk in range(chunks):
+        finish(1, chunk, send2, recv2)
+        x = recv2[chunk].reshape(devices, half, sub, size)
+        x = exchange(x, 0, [(k, k) for k in range(top)])
+        x = x.reshape(seven, devices // seven, half, sub, size)
+        for p in range(seven):
+            for e in range(half):
+                tmp[:, (e * seven + p) * sub : (e * seven + p + 1) * sub, :] = x[p, :, e]
+        flat = tmp.reshape(devices // seven * mid * sub, size)
+        for hi in range(devices // seven):
+            for w in range(low):
+                for c in range(2):
+                    rows = flat[pl.ds(hi * mid * sub + w * 2 + c, mid, stride=sub), :]
+                    at = chunk * span + (hi * low + w) * 2 * mid + c
+                    o_ref[pl.ds(at, mid, stride=2), :] = rows
+
+
+def square(mixer, dims, order, columns=True):
+    count = len(dims)
+    block = blocked(mixer).reshape((2,) + dims + (2,) + dims)
+    perm = tuple(k + 1 for k in order)
+    second = tuple(k + 1 + count for k in perm) if columns else tuple(range(count + 1, 2 * count + 2))
+    wide = 2 * mixer.shape[-1]
+    return block.transpose(perm + second).reshape(wide, wide)
+
+
+def fast_body(state, gates, n_group, n_inner):
+    size = gates.shape[-1]
+    total = state.shape[1]
+    devices = n_group * n_inner
+    rest = low = size // devices
+    half = size // n_group // low
+    mid = total // size // size
+    seven = mid // half
+    mul = functools.partial(jnp.matmul, precision=lax.Precision.HIGHEST)
+    wide = 2 * size
+    merged = mul(
+        blocked(gates[5]).reshape(wide, wide),
+        mul(blocked(gates[3]).reshape(wide, wide), blocked(gates[0]).reshape(wide, wide)),
+    )
+    merged = merged.reshape(2, rest, devices, wide).transpose(2, 0, 1, 3).reshape(wide, wide)
+    w = jnp.stack(
+        [
+            square(gates[1], (2, n_inner // 2, n_group, low), (-1, 0, 3, 1, 2), False),
+            merged,
+            square(gates[2], (n_inner, n_group, low), (1, 0, 2, -1)),
+            square(gates[4], (n_group, low, half), (2, 0, 1, -1)),
+            square(gates[6], (n_inner, n_group, low), (1, 0, 2, -1)),
+            square(gates[7], (low, half, seven, rest), (1, 3, 2, 0, -1)),
+        ]
+    )
+    x = state.reshape(2, total // size, size).transpose(1, 0, 2).reshape(-1, size)
+    chunk = (2, devices, x.shape[0] // 2 // devices, size)
+    vmem = pl.BlockSpec(memory_space=pltpu.VMEM)
+    out = pl.pallas_call(
+        functools.partial(kernel, n_group, n_inner),
+        out_shape=jax.ShapeDtypeStruct(x.shape, F32),
+        in_specs=[vmem, vmem],
+        out_specs=vmem,
+        scratch_shapes=[
+            pltpu.VMEM(chunk, F32),
+            pltpu.VMEM(chunk, F32),
+            pltpu.VMEM(chunk, F32),
+            pltpu.VMEM(chunk, F32),
+            pltpu.VMEM((devices // seven, mid * 2 * low, size), F32),
+            pltpu.VMEM((w.shape[0], 2, wide, wide), BF16),
+            pltpu.SemaphoreType.DMA((2, 2, devices)),
+            pltpu.SemaphoreType.DMA((2, 2, devices)),
+        ],
+        compiler_params=pltpu.CompilerParams(
+            collective_id=0, has_side_effects=True, vmem_limit_bytes=40 << 20
+        ),
+    )(x, w)
+    return out.reshape(total // size, 2, size).transpose(1, 0, 2).reshape(2, total)
+
+
 def solution(mesh):
+    n_inner, n_group = mesh.shape["inner"], mesh.shape["group"]
+
+    def body(state, gates):
+        size, total = gates.shape[-1], state.shape[1]
+        gate_bits, local_bits = size.bit_length() - 1, total.bit_length() - 1
+        inner_bits = n_inner.bit_length() - 1
+        device_bits = inner_bits + n_group.bit_length() - 1
+        upper = local_bits - gate_bits
+        fits = (
+            device_bits == upper // 2
+            and upper // 2 + gate_bits == local_bits - device_bits
+            and upper - inner_bits >= gate_bits
+        )
+        if fits:
+            return fast_body(state, gates, n_group, n_inner)
+        return general_body(state, gates)
+
     in_specs = (P(None, ("group", "inner")), P())
     out_specs = P(None, ("group", "inner"))
     return jax.shard_map(body, mesh=mesh, in_specs=in_specs, out_specs=out_specs, check_vma=False)

time: 140 us -> 469 us (3.35)
  the two profiles are of different devices: /device:TPU:0 before, /device:TPU:15 now
where the time goes in v1:
time: 469 us; the launch traced here: 465 us
  local copies, waits for them, and re-layouts  356 us (76%)
  Pallas kernels  55.2 us (12%)
  other arithmetic  52.3 us (11%)
    transpose x5, local copies, waits for them, and re-layouts, square(): return block.transpose(perm + second).reshape(wide, wide)  234 us
    another operation x8, local copies, waits for them, and re-layouts, fast_body(): jnp.stack([square(gates[1], (2, n_inner // 2, n_group, low), (-1, 0, 3, 1...  78.4 us
    pallas_call x1, Pallas kernels, fast_body(): pl.pallas_call(functools.partial(kernel, n_group, n_inner), out_shape=jax...  55.2 us
    transpose x5, other arithmetic, square(): return block.transpose(perm + second).reshape(wide, wide)  34.3 us
    another operation x7, local copies, waits for them, and re-layouts, blocked(): jnp.stack([real_part, -imag_part], 1)  21.6 us
    neg x6, other arithmetic, blocked(): -imag_part  17.9 us
    squeeze x5, local copies, waits for them, and re-layouts, blocked(): imag_part = mixer[1]  17.7 us

profile of v1, /device:TPU:15, one launch (start us, length us, event | category | flops | bytes accessed | tf_op | source)
XLA Modules:
  0.0 464.7 jit_solution(2844796899030229733)
XLA Ops:
  0.0 1.3 fusion.11
  1.3 0.9 fusion.8
  2.3 0.2 copy.61
  2.6 0.2 copy.62
  2.8 0.4 convolution_bitcast_fusion.1
  3.2 0.1 copy.59
  3.3 0.1 stack.126
  3.4 0.1 copy.60
  3.5 0.1 stack.128
  3.6 0.4 convolution_bitcast_fusion
  4.0 0.2 copy.63
  4.2 0.1 stack_reshape.19
  4.3 2.1 squeeze.32
  6.5 1.6 neg.85
  8.1 3.5 stack.121
  11.6 6.6 %maximum_bitcast_fusion = f32[2,2,4,2,8,2,2,2,8,4]{9,8,7,6,2,4,3,1,5,0:T(8,128)} fusion(f32[1,2,2,8,4,1,2,2,8,4]{9,8,7,6,4,3,2,1,5,0:T(8,128)} %stack.121, f32[1,2,2,8,4,1,2,2,8,4]{9,8,7,6,4,3,2,1,5,0:T(8,128)S(1)} %squeeze.32, f32[1,2,2,8,4,1,2,2,8,4]{9,8,7,6,4,3,2,1,5,0:T(8,128)} %neg.85), kind=kLoop, calls=%fused_computation | loop fusion | flops 196608 | bytes 458752 | tf_op jit(solution)/shard_map/transpose | solution.py:235
  18.2 17.0 %copy.58 = f32[2,2,4,2,8,2,2,2,8,4]{4,3,2,1,0,9,8,7,6,5:T(2,128)} copy(f32[2,2,4,2,8,2,2,2,8,4]{9,8,7,6,2,4,3,1,5,0:T(8,128)} %maximum_bitcast_fusion) | data formatting | bytes 524288 | tf_op jit(solution)/shard_map/transpose | solution.py:235
  35.2 7.8 %stack_reshape.18 = f32[1,256,256]{1,2,0:T(8,128)S(1)} reshape(f32[2,2,4,2,8,2,2,2,8,4]{4,3,2,1,0,9,8,7,6,5:T(2,128)} %copy.58) | data formatting | bytes 524288 | tf_op jit(solution)/shard_map/stack;reshape | solution.py:253
  43.0 0.1 copy.72
  43.2 3.5 squeeze.36
  46.7 3.3 neg.89
  49.9 3.5 stack.140
  53.4 7.4 %maximum_bitcast_fusion.1 = f32[8,4,4,2,8,4,4,2]{6,4,5,2,0,1,7,3:T(8,128)} fusion(f32[1,4,8,4,1,4,8,4]{7,6,5,3,2,1,4,0:T(8,128)} %stack.140, f32[1,4,8,4,1,4,8,4]{7,6,5,3,2,1,4,0:T(8,128)} %squeeze.36, f32[1,4,8,4,1,4,8,4]{7,6,5,3,2,1,4,0:T(8,128)} %neg.89), kind=kLoop, calls=%fused_computation.1 | loop fusion | flops 196608 | bytes 458752 | tf_op jit(solution)/shard_map/transpose | solution.py:235
  60.8 51.7 %copy.64 = f32[8,4,4,2,8,4,4,2]{7,6,5,4,3,2,1,0:T(4,128)} copy(f32[8,4,4,2,8,4,4,2]{6,4,5,2,0,1,7,3:T(8,128)} %maximum_bitcast_fusion.1) | data formatting | bytes 524288 | tf_op jit(solution)/shard_map/transpose | solution.py:235
  112.5 17.6 %stack_reshape.20 = f32[1,256,256]{2,1,0:T(8,128)S(1)} reshape(f32[8,4,4,2,8,4,4,2]{7,6,5,4,3,2,1,0:T(4,128)} %copy.64) | data formatting | bytes 524288 | tf_op jit(solution)/shard_map/stack;reshape | solution.py:253
  130.1 4.0 squeeze.37
  134.2 3.8 neg.90
  137.9 4.1 stack.144
  142.0 8.5 %maximum_bitcast_fusion.2 = f32[4,8,4,2,4,8,4,2]{4,6,5,0,2,1,7,3:T(4,128)} fusion(f32[1,8,4,4,1,8,4,4]{7,6,5,3,2,1,4,0:T(4,128)} %stack.144, f32[1,8,4,4,1,8,4,4]{7,6,5,3,2,1,4,0:T(4,128)} %squeeze.37, f32[1,8,4,4,1,8,4,4]{7,6,5,3,2,1,4,0:T(4,128)} %neg.90), kind=kLoop, calls=%fused_computation.2 | loop fusion | flops 196608 | bytes 458752 | tf_op jit(solution)/shard_map/transpose | solution.py:235
  150.5 60.9 %copy.65 = f32[4,8,4,2,4,8,4,2]{7,6,5,4,3,2,1,0:T(4,128)} copy(f32[4,8,4,2,4,8,4,2]{4,6,5,0,2,1,7,3:T(4,128)} %maximum_bitcast_fusion.2) | data formatting | bytes 524288 | tf_op jit(solution)/shard_map/transpose | solution.py:235
  211.4 17.4 %stack_reshape.21 = f32[1,256,256]{2,1,0:T(8,128)S(1)} reshape(f32[4,8,4,2,4,8,4,2]{7,6,5,4,3,2,1,0:T(4,128)} %copy.65) | data formatting | bytes 524288 | tf_op jit(solution)/shard_map/stack;reshape | solution.py:253
  228.8 3.5 squeeze.38
  232.3 3.3 neg.91
  235.5 3.5 stack.148
  239.1 7.4 %maximum_bitcast_fusion.3 = f32[8,4,4,2,8,4,4,2]{6,4,5,2,0,1,7,3:T(8,128)} fusion(f32[1,4,8,4,1,4,8,4]{7,6,5,3,2,1,4,0:T(8,128)} %stack.148, f32[1,4,8,4,1,4,8,4]{7,6,5,3,2,1,4,0:T(8,128)} %squeeze.38, f32[1,4,8,4,1,4,8,4]{7,6,5,3,2,1,4,0:T(8,128)} %neg.91), kind=kLoop, calls=%fused_computation.3 | loop fusion | flops 196608 | bytes 458752 | tf_op jit(solution)/shard_map/transpose | solution.py:235
  246.4 51.7 %copy.66 = f32[8,4,4,2,8,4,4,2]{7,6,5,4,3,2,1,0:T(4,128)} copy(f32[8,4,4,2,8,4,4,2]{6,4,5,2,0,1,7,3:T(8,128)} %maximum_bitcast_fusion.3) | data formatting | bytes 524288 | tf_op jit(solution)/shard_map/transpose | solution.py:235
  298.1 17.8 %stack_reshape.22 = f32[1,256,256]{2,1,0:T(8,128)S(1)} reshape(f32[8,4,4,2,8,4,4,2]{7,6,5,4,3,2,1,0:T(4,128)} %copy.66) | data formatting | bytes 524288 | tf_op jit(solution)/shard_map/stack;reshape | solution.py:253
  315.9 4.6 squeeze.39
  320.5 5.1 %copy_negate_fusion = (f32[1,4,4,2,4,1,4,4,2,4]{9,7,8,6,5,4,3,2,1,0:T(4,128)}, f32[1,4,4,2,4,1,4,4,2,4]{9,7,8,6,5,4,3,2,1,0:T(4,128)}) fusion(f32[1,4,4,2,4,1,4,4,2,4]{9,8,7,6,4,3,2,1,5,0:T(2,128)} %squeeze.39), kind=kLoop, calls=%fused_computation.38 | loop fusion | flops 16384 | bytes 196608 | tf_op jit(solution)/shard_map/neg | solution.py:15
  325.6 4.6 stack.152
  330.1 0.0 copy-start.1
  330.1 0.0 copy-start.2
  330.1 2.3 copy.68
  332.4 0.0 copy-done.1
  332.4 0.5 copy-done.2
  333.0 4.5 maximum_bitcast_fusion.4
  337.4 53.3 %copy.71 = f32[4,4,2,4,2,4,4,2,4,2]{9,8,7,6,5,4,3,2,1,0:T(4,128)} copy(f32[4,4,2,4,2,4,4,2,4,2]{6,5,7,8,9,1,2,0,3,4:T(4,128)} %maximum_bitcast_fusion.4) | data formatting | bytes 524288 | tf_op jit(solution)/shard_map/transpose | solution.py:235
  390.7 0.0 copy-start
  390.7 17.5 %stack_reshape.23 = f32[1,256,256]{2,1,0:T(8,128)S(1)} reshape(f32[4,4,2,4,2,4,4,2,4,2]{9,8,7,6,5,4,3,2,1,0:T(4,128)} %copy.71) | data formatting | bytes 524288 | tf_op jit(solution)/shard_map/stack;reshape | solution.py:253
  408.3 0.0 copy-done
  408.3 55.2 %shard_map.28 = f32[2048,128]{1,0:T(8,128)S(1)} custom-call(f32[2048,128]{1,0:T(8,128)S(1)} %bitcast.86, f32[6,256,256]{2,1,0:T(8,128)S(1)} %constant_dynamic-update-slice_fusion.w_ref), custom_call_target="tpu_custom_call" | custom-call | tf_op jit(solution)/shard_map/pallas_call | solution.py:266
  463.5 1.0 copy.93
  (10 shorter events, 0.2 us)
Async XLA Ops:
  330.1 2.3 copy-start.1
  330.1 2.9 copy-start.2
  390.7 17.5 %copy-start = (f32[2,131072]{1,0:T(2,128)S(1)}, f32[2,131072]{1,0:T(2,128)}, u32[]{:S(2)}) copy-start(f32[2,131072]{1,0:T(2,128)} %param.2) | copy-start | bytes 3145732

commit v2 on v1

--- a/solution.py
+++ b/solution.py
@@ -93,8 +93,18 @@
     return x
 
 
+def order_index(index, dims, order):
+    bits = [d.bit_length() - 1 for d in dims]
+    source, low = 0, 0
+    for axis in reversed(order):
+        digit = (index >> low) & (dims[axis] - 1)
+        source = source + (digit << sum(bits[axis + 1 :]))
+        low += bits[axis]
+    return source
+
+
 def kernel(
-    n_group, n_inner, x_ref, w_ref, o_ref, send1, recv1, send2, recv2, tmp, weights, ssem, rsem
+    n_group, n_inner, x_ref, g_ref, o_ref, send1, recv1, send2, recv2, tmp, weights, ssem, rsem
 ):
     devices = n_group * n_inner
     size = x_ref.shape[1]
@@ -121,8 +131,27 @@
             barrier, inc=1, device_id=peer(step)[1], device_id_type=pl.DeviceIdType.MESH
         )
 
-    for k in range(w_ref.shape[0]):
-        weights[k, 0], weights[k, 1] = split(w_ref[k])
+    def gate(k):
+        re, im = g_ref[k, 0], g_ref[k, 1]
+        return jnp.concatenate(
+            [jnp.concatenate([re, -im], axis=1), jnp.concatenate([im, re], axis=1)], axis=0
+        )
+
+    def place(k, matrix, order, columns=True):
+        for part, piece in enumerate(split(matrix)):
+            piece = select(order, piece)
+            if columns:
+                piece = select(order, piece, False)
+            weights[k, part] = piece.astype(BF16)
+
+    def select(order, piece, rows=True):
+        shape = (wide, wide)
+        source = order_index(lax.broadcasted_iota(jnp.int32, shape, 0), *order)
+        hit = source == lax.broadcasted_iota(jnp.int32, shape, 1)
+        ones = jnp.where(hit, 1.0, 0.0).astype(BF16)
+        left, right = (ones, piece) if rows else (piece.astype(BF16), ones)
+        dims = (((1,), (0 if rows else 1,)), ((), ()))
+        return lax.dot_general(left, right, dims, preferred_element_type=F32)
 
     def weight(k):
         return weights[k, 0], weights[k, 1]
@@ -149,6 +178,11 @@
         @pl.loop(1, devices)
         def _(step):
             copies(swap, chunk, step, source, landing).wait()
+
+    place(0, gate(1), ((2, chunks, n_inner // chunks, n_group, low), (0, 1, 4, 2, 3)), False)
+    merged = dot3(split(gate(3)), split(gate(0)))
+    merged = dot3(split(gate(5)), split(merged))
+    place(1, merged, ((2, rest, devices), (2, 0, 1)), False)
 
     cols = [
         jnp.concatenate(
@@ -171,6 +205,11 @@
             piece = z[:, w * size : (w + 1) * size].reshape(devices, 2 * rest, size)
             send1[chunk, :, w * 2 * rest : (w + 1) * 2 * rest, :] = piece
         start(0, chunk, send1, recv1)
+
+    place(2, gate(2), ((2, n_inner, n_group, low), (2, 1, 3, 0)))
+    place(3, gate(4), ((2, n_group, low, half), (3, 1, 2, 0)))
+    place(4, gate(6), ((2, n_inner, n_group, low), (2, 1, 3, 0)))
+    place(5, gate(7), ((2, low, half, seven, rest), (2, 4, 3, 1, 0)))
 
     bits_t = range(n_group.bit_length() - 1)
     lane_bits = size.bit_length() - 1
@@ -226,40 +265,15 @@
                     o_ref[pl.ds(at, mid, stride=2), :] = rows
 
 
-def square(mixer, dims, order, columns=True):
-    count = len(dims)
-    block = blocked(mixer).reshape((2,) + dims + (2,) + dims)
-    perm = tuple(k + 1 for k in order)
-    second = tuple(k + 1 + count for k in perm) if columns else tuple(range(count + 1, 2 * count + 2))
-    wide = 2 * mixer.shape[-1]
-    return block.transpose(perm + second).reshape(wide, wide)
-
-
 def fast_body(state, gates, n_group, n_inner):
     size = gates.shape[-1]
     total = state.shape[1]
     devices = n_group * n_inner
-    rest = low = size // devices
+    low = size // devices
     half = size // n_group // low
     mid = total // size // size
     seven = mid // half
-    mul = functools.partial(jnp.matmul, precision=lax.Precision.HIGHEST)
     wide = 2 * size
-    merged = mul(
-        blocked(gates[5]).reshape(wide, wide),
-        mul(blocked(gates[3]).reshape(wide, wide), blocked(gates[0]).reshape(wide, wide)),
-    )
-    merged = merged.reshape(2, rest, devices, wide).transpose(2, 0, 1, 3).reshape(wide, wide)
-    w = jnp.stack(
-        [
-            square(gates[1], (2, n_inner // 2, n_group, low), (-1, 0, 3, 1, 2), False),
-            merged,
-            square(gates[2], (n_inner, n_group, low), (1, 0, 2, -1)),
-            square(gates[4], (n_group, low, half), (2, 0, 1, -1)),
-            square(gates[6], (n_inner, n_group, low), (1, 0, 2, -1)),
-            square(gates[7], (low, half, seven, rest), (1, 3, 2, 0, -1)),
-        ]
-    )
     x = state.reshape(2, total // size, size).transpose(1, 0, 2).reshape(-1, size)
     chunk = (2, devices, x.shape[0] // 2 // devices, size)
     vmem = pl.BlockSpec(memory_space=pltpu.VMEM)
@@ -274,14 +288,14 @@
             pltpu.VMEM(chunk, F32),
             pltpu.VMEM(chunk, F32),
             pltpu.VMEM((devices // seven, mid * 2 * low, size), F32),
-            pltpu.VMEM((w.shape[0], 2, wide, wide), BF16),
+            pltpu.VMEM((6, 2, wide, wide), BF16),
             pltpu.SemaphoreType.DMA((2, 2, devices)),
             pltpu.SemaphoreType.DMA((2, 2, devices)),
         ],
         compiler_params=pltpu.CompilerParams(
             collective_id=0, has_side_effects=True, vmem_limit_bytes=40 << 20
         ),
-    )(x, w)
+    )(x, gates)
     return out.reshape(total // size, 2, size).transpose(1, 0, 2).reshape(2, total)
 
 

time: 469 us -> 58.6 us (0.12)
  local copies, waits for them, and re-layouts: 356 us -> 3.42 us
  other arithmetic: 52.3 us -> 0 us
    transpose x6 -> x0, local copies, waits for them, and re-layouts: 235 us -> none  [the longest x5 234 us: square(): return block.transpose(perm + second).reshape(wide, wide)]
    another operation x20 -> x0, local copies, waits for them, and re-layouts: 101 us -> none  [the longest x8 78.4 us: fast_body(): jnp.stack([square(gates[1], (2, n_inner // 2, n_group, low), (-1, 0, 3, 1...]
    transpose x5 -> x0, other arithmetic: 34.3 us -> none  [square(): return block.transpose(perm + second).reshape(wide, wide)]
    neg x6 -> x0, other arithmetic: 17.9 us -> none  [blocked(): -imag_part]
    squeeze x5 -> x0, local copies, waits for them, and re-layouts: 17.7 us -> none  [blocked(): imag_part = mixer[1]]
where the time goes in v2:
time: 58.6 us; the launch traced here: 58.4 us
  Pallas kernels  54.9 us (94%)
  local copies, waits for them, and re-layouts  3.42 us (6%)
    pallas_call x1, Pallas kernels, fast_body(): pl.pallas_call(functools.partial(kernel, n_group, n_inner), out_shape=jax...  54.9 us
    unnamed x5, local copies, waits for them, and re-layouts  3.42 us

profile of v2, /device:TPU:15, one launch (start us, length us, event | category | flops | bytes accessed | tf_op | source)
XLA Modules:
  0.0 58.4 jit_solution(13244690600104059098)
XLA Ops:
  0.0 0.0 copy-start
  0.0 1.2 %copy-done = f32[2,131072]{1,0:T(2,128)S(1)} copy-done((f32[2,131072]{1,0:T(2,128)S(1)}, f32[2,131072]{1,0:T(2,128)}, u32[]{:S(2)}) %copy-start) | copy-done | bytes 1048600
  1.2 0.0 copy-start.1
  1.2 1.2 %copy-done.1 = f32[8,2,128,128]{3,2,1,0:T(8,128)S(1)} copy-done((f32[8,2,128,128]{3,2,1,0:T(8,128)S(1)}, f32[8,2,128,128]{3,2,1,0:T(8,128)}, u32[]{:S(2)}) %copy-start.1) | copy-done | bytes 1048600
  2.5 54.9 %shard_map.28 = f32[2048,128]{1,0:T(8,128)S(1)} custom-call(f32[2048,128]{1,0:T(8,128)S(1)} %bitcast.11, f32[8,2,128,128]{3,2,1,0:T(8,128)S(1)} %copy-done.1), custom_call_target="tpu_custom_call" | custom-call | tf_op jit(solution)/shard_map/pallas_call | solution.py:280
  57.4 1.0 %copy.6 = f32[2,131072]{1,0:T(2,128)} copy(f32[2,131072]{1,0:T(2,128)S(1)} %bitcast.10) | data formatting | bytes 2097152
Async XLA Ops:
  0.0 1.2 %copy-start = (f32[2,131072]{1,0:T(2,128)S(1)}, f32[2,131072]{1,0:T(2,128)}, u32[]{:S(2)}) copy-start(f32[2,131072]{1,0:T(2,128)} %param.2) | copy-start | bytes 3145732
  1.2 1.2 %copy-start.1 = (f32[8,2,128,128]{3,2,1,0:T(8,128)S(1)}, f32[8,2,128,128]{3,2,1,0:T(8,128)}, u32[]{:S(2)}) copy-start(f32[8,2,128,128]{3,2,1,0:T(8,128)} %g_ref.1) | copy-start | bytes 3145732

commit v3 on v2

--- a/solution.py
+++ b/solution.py
@@ -104,7 +104,22 @@
 
 
 def kernel(
-    n_group, n_inner, x_ref, g_ref, o_ref, send1, recv1, send2, recv2, tmp, weights, ssem, rsem
+    n_group,
+    n_inner,
+    x_hbm,
+    g_hbm,
+    o_ref,
+    x_ref,
+    g_ref,
+    send1,
+    recv1,
+    send2,
+    recv2,
+    tmp,
+    weights,
+    ssem,
+    rsem,
+    lsem,
 ):
     devices = n_group * n_inner
     size = x_ref.shape[1]
@@ -123,6 +138,10 @@
         other = lax.rem(me + step, devices)
         return other, (other // n_inner, lax.rem(other, n_inner))
 
+    load_g = pltpu.make_async_copy(g_hbm, g_ref, lsem.at[0])
+    load_x = pltpu.make_async_copy(x_hbm, x_ref, lsem.at[1])
+    load_g.start()
+    load_x.start()
     barrier = pltpu.get_barrier_semaphore()
 
     @pl.loop(1, devices)
@@ -179,10 +198,13 @@
         def _(step):
             copies(swap, chunk, step, source, landing).wait()
 
+    load_g.wait()
     place(0, gate(1), ((2, chunks, n_inner // chunks, n_group, low), (0, 1, 4, 2, 3)), False)
     merged = dot3(split(gate(3)), split(gate(0)))
     merged = dot3(split(gate(5)), split(merged))
     place(1, merged, ((2, rest, devices), (2, 0, 1)), False)
+
+    load_x.wait()
 
     cols = [
         jnp.concatenate(
@@ -280,9 +302,11 @@
     out = pl.pallas_call(
         functools.partial(kernel, n_group, n_inner),
         out_shape=jax.ShapeDtypeStruct(x.shape, F32),
-        in_specs=[vmem, vmem],
+        in_specs=[pl.BlockSpec(memory_space=pltpu.HBM)] * 2,
         out_specs=vmem,
         scratch_shapes=[
+            pltpu.VMEM(x.shape, F32),
+            pltpu.VMEM(gates.shape, F32),
             pltpu.VMEM(chunk, F32),
             pltpu.VMEM(chunk, F32),
             pltpu.VMEM(chunk, F32),
@@ -291,9 +315,10 @@
             pltpu.VMEM((6, 2, wide, wide), BF16),
             pltpu.SemaphoreType.DMA((2, 2, devices)),
             pltpu.SemaphoreType.DMA((2, 2, devices)),
+            pltpu.SemaphoreType.DMA((2,)),
         ],
         compiler_params=pltpu.CompilerParams(
-            collective_id=0, has_side_effects=True, vmem_limit_bytes=40 << 20
+            collective_id=0, has_side_effects=True, vmem_limit_bytes=52 << 20
         ),
     )(x, gates)
     return out.reshape(total // size, 2, size).transpose(1, 0, 2).reshape(2, total)

time: 58.6 us -> 56.2 us (0.959)
  local copies, waits for them, and re-layouts: 3.42 us -> 0.97 us
    unnamed x5 -> x1, local copies, waits for them, and re-layouts: 3.42 us -> 0.97 us
where the time goes in v3:
time: 56.2 us; the launch traced here: 56 us
  Pallas kernels  55.1 us (98%)
  local copies, waits for them, and re-layouts  0.97 us (2%)
    pallas_call x1, Pallas kernels, fast_body(): pl.pallas_call(functools.partial(kernel, n_group, n_inner), out_shape=jax...  55.1 us

profile of v3, /device:TPU:15, one launch (start us, length us, event | category | flops | bytes accessed | tf_op | source)
XLA Modules:
  0.0 56.0 jit_solution(2735446322078309283)
XLA Ops:
  0.0 55.1 %shard_map.28 = f32[2048,128]{1,0:T(8,128)S(1)} custom-call(f32[2048,128]{1,0:T(8,128)} %bitcast.11, f32[8,2,128,128]{3,2,1,0:T(8,128)} %g_hbm.1), custom_call_target="tpu_custom_call" | custom-call | tf_op jit(solution)/shard_map/pallas_call | solution.py:302
  55.1 1.0 %copy.6 = f32[2,131072]{1,0:T(2,128)} copy(f32[2,131072]{1,0:T(2,128)S(1)} %bitcast.10) | data formatting | bytes 2097152

commit v4 on v3

--- a/solution.py
+++ b/solution.py
@@ -219,13 +219,14 @@
     ]
     y = jnp.stack(tiles, 3)
     y = y.reshape(2, chunks, low * size, size)
-    pl.semaphore_wait(barrier, devices - 1)
     for chunk in range(chunks):
         rows = jnp.concatenate([y[0, chunk], y[1, chunk]], axis=1)
         z = dot3(weight(1), split(rows), True)
         for w in range(low):
             piece = z[:, w * size : (w + 1) * size].reshape(devices, 2 * rest, size)
             send1[chunk, :, w * 2 * rest : (w + 1) * 2 * rest, :] = piece
+        if chunk == 0:
+            pl.semaphore_wait(barrier, devices - 1)
         start(0, chunk, send1, recv1)
 
     place(2, gate(2), ((2, n_inner, n_group, low), (2, 1, 3, 0)))

time: 56.2 us -> 56.1 us (level); the launches traced: 56 us -> 55.3 us
  Pallas kernels: 55.1 us -> 54.3 us
    pallas_call x1, Pallas kernels: 55.1 us -> 54.3 us  [fast_body(): pl.pallas_call(functools.partial(kernel, n_group, n_inner), out_shape=jax...]
where the time goes in v4:
time: 56.1 us; the launch traced here: 55.3 us
  Pallas kernels  54.3 us (97%)
  local copies, waits for them, and re-layouts  0.97 us (2%)
    pallas_call x1, Pallas kernels, fast_body(): pl.pallas_call(functools.partial(kernel, n_group, n_inner), out_shape=jax...  54.3 us

profile of v4, /device:TPU:15, one launch (start us, length us, event | category | flops | bytes accessed | tf_op | source)
XLA Modules:
  0.0 55.3 jit_solution(1465572225327152988)
XLA Ops:
  0.0 54.3 %shard_map.28 = f32[2048,128]{1,0:T(8,128)S(1)} custom-call(f32[2048,128]{1,0:T(8,128)} %bitcast.11, f32[8,2,128,128]{3,2,1,0:T(8,128)} %g_hbm.1), custom_call_target="tpu_custom_call" | custom-call | tf_op jit(solution)/shard_map/pallas_call | solution.py:303
  54.4 1.0 %copy.6 = f32[2,131072]{1,0:T(2,128)} copy(f32[2,131072]{1,0:T(2,128)S(1)} %bitcast.10) | data formatting | bytes 2097152
